TPU v7x, 32 devices: a whole 2x2x4 slice. The times are simulated.
32 devices in a mesh: branch: 2 (over x), tok: 16 (over z, y, core).
Axes of the slice: x: 2, y: 2, z: 4, core: 2. Of those that a mesh axis runs over, the one named last changes fastest.
Arguments:
- teacher_hidden: bfloat16 [2, 256, 4096], P('branch', 'tok'), may hold values from -400 to 400
- teacher_gain: float32 [2, 4096], P('branch'), may hold values from 0.5 to 1.5
- teacher_head: bfloat16 [2, 4096, 20480], P('branch', None, 'tok'), may hold values from -30 to 30
- student_hidden: bfloat16 [256, 4096], P('branch'), may hold values from -400 to 400
- student_gain: float32 [4096], replicated, may hold values from 0.5 to 1.5
- student_head: bfloat16 [4096, 20480], P('branch', 'tok'), may hold values from -30 to 30
- cluster_weights: int32 [256, 2], P(None, 'branch'), may hold values from 0 to 64, as said below
- token_ids: int32 [256], P('branch'), may hold values from 0 to 20479
Outputs:
- grad_head: float32 [4096, 20480], P('branch', 'tok')
- grad_hidden: float32 [256, 4096], P('branch', 'tok')
- grad_gain: float32 [4096], P('tok')
Inputs may be any that keep to these rules, and one draw needn't show every extreme that they name: `cluster_weights`: each token's 2 weights sum to 64.
All inputs are finite; a program needn't handle non-finite values.
Results may differ from a plain program's by a relative error of at most 0.0063.
Values may be sent and summed in bfloat16 or wider, within the bound.
No kernel may reach another device: no remote copies, remote signals or barrier semaphores. Data moves between devices by JAX's collectives and lax.ppermute only.
A program may use at most 128 MiB of HBM per device.

v0:
```python
import jax
import jax.numpy as jnp
from jax import lax
from jax.sharding import PartitionSpec as P

DEN = 64
eps = 1e-05
mix_label = 0.25
loss_scale = 64.0


def merged(value, axis, combine):
    everything = jax.tree.map(lambda part: lax.all_gather(part, axis), value)
    leading = jax.tree.map(lambda part: part[0], everything)

    def step(k, so_far):
        return combine(so_far, jax.tree.map(lambda part: part[k], everything))

    return lax.fori_loop(1, lax.axis_size(axis), step, leading)


def normalize(hidden, gain):
    values = hidden.astype(jnp.float32)
    inv_scale = lax.rsqrt(jnp.mean(values * values, axis=-1, keepdims=True) + eps)
    return ((values * inv_scale * gain).astype(jnp.bfloat16), inv_scale)


def combine_stats(first, second):
    top = jnp.maximum(first[0], second[0])
    return (top, first[1] * jnp.exp(first[0] - top) + second[1] * jnp.exp(second[0] - top))


def probabilities(logits):
    local_max = jnp.max(logits, axis=1)
    local_scaled = jnp.exp(logits - local_max[:, None])
    row_max, row_total = merged((local_max, jnp.sum(local_scaled, axis=1)), "tok", combine_stats)
    scaled = local_scaled * jnp.exp(local_max - row_max)[:, None]
    return scaled / row_total[:, None]


def per_device(
    teacher_hidden,
    teacher_gain,
    teacher_head,
    student_hidden,
    student_gain,
    student_head,
    cluster_weights,
    token_ids,
):
    rows_here = student_hidden.shape[0]
    width = student_hidden.shape[1]
    head_cols = teacher_head.shape[2]
    branch_gain = teacher_gain[0]
    branch_head = teacher_head[0]
    normed, unused_scale = normalize(
        lax.all_gather(teacher_hidden[0], "tok", axis=0, tiled=True), branch_gain
    )
    teacher_logits = jnp.dot(normed, branch_head, preferred_element_type=jnp.float32)
    weight = cluster_weights[:, 0].astype(jnp.float32) / DEN
    terms = probabilities(teacher_logits) * weight[:, None]
    mixed_all = lax.psum(terms, "branch")
    mixed = lax.dynamic_slice_in_dim(mixed_all, lax.axis_index("branch") * rows_here, rows_here, 0)
    student_normed, inv_scale = normalize(student_hidden, student_gain)
    student_logits = jnp.dot(
        student_normed,
        lax.all_gather(student_head, "branch", axis=0, tiled=True),
        preferred_element_type=jnp.float32,
    )
    student_probs = probabilities(student_logits)
    offset = lax.axis_index("tok") * head_cols
    onehot = (
        token_ids[:, None] == offset + jnp.arange(head_cols, dtype=jnp.int32)[None, :]
    ).astype(jnp.float32)
    targets = (1.0 - mix_label) * mixed + mix_label * onehot
    logit_grads = (loss_scale * (student_probs - targets)).astype(jnp.bfloat16)
    contract = (((1,), (1,)), ((), ()))
    partial_grads = lax.dot_general(
        logit_grads,
        lax.all_gather(student_head, "branch", axis=0, tiled=True),
        contract,
        preferred_element_type=jnp.float32,
    )
    normed_grads = lax.psum_scatter(partial_grads, "tok", scatter_dimension=1, tiled=True)
    slice_width = normed_grads.shape[1]
    col_start = lax.axis_index("tok") * slice_width
    hidden_cols = lax.dynamic_slice_in_dim(student_hidden, col_start, slice_width, 1).astype(
        jnp.float32
    )
    gain_cols = lax.dynamic_slice_in_dim(student_gain, col_start, slice_width, 0)
    grad_gain = lax.psum(jnp.sum(normed_grads * hidden_cols * inv_scale, axis=0), "branch")
    row_dots = lax.psum(jnp.sum(gain_cols[None, :] * normed_grads * hidden_cols, axis=1), "tok")
    grad_hidden = (
        inv_scale * gain_cols[None, :] * normed_grads
        - hidden_cols * inv_scale**3 * row_dots[:, None] / width
    )
    exchanged = lax.all_to_all(student_normed, "branch", split_axis=1, concat_axis=0, tiled=True)
    all_grads = lax.all_gather(logit_grads, "branch", axis=0, tiled=True)
    grad_head = lax.dot_general(
        exchanged, all_grads, (((0,), (0,)), ((), ())), preferred_element_type=jnp.float32
    )
    return (grad_head, grad_hidden, grad_gain)


def solution(mesh):
    in_specs = (
        P("branch", "tok", None),
        P("branch", None),
        P("branch", None, "tok"),
        P("branch", None),
        P(),
        P("branch", "tok"),
        P(None, "branch"),
        P("branch"),
    )
    out_specs = (P("branch", "tok"), P("branch", "tok"), P("tok"))
    return jax.shard_map(
        per_device, mesh=mesh, in_specs=in_specs, out_specs=out_specs, check_vma=False
    )
```

profile of v0, /device:TPU:0, one launch (start us, length us, event | category | flops | bytes accessed | tf_op | source)
XLA Modules:
  0.0 349.2 jit_solution(5427056235205396135)
XLA Ops:
  7.2 0.0 all-gather.14.cloned.1.call-start
  7.2 0.7 all-gather.14.cloned.1.call-update
  7.9 0.0 copy-start.1
  7.9 0.0 all-gather.12.cloned.1.call-start
  8.0 0.7 all-gather.12.cloned.1.call-update
  8.7 0.0 copy-start.3
  8.7 0.0 copy-start.2
  8.7 0.0 all-reduce.2.cloned.1.call-start
  8.7 0.4 copy-done.1
  9.1 0.7 copy.13
  9.8 0.6 fusion.7
  10.4 0.0 copy-done.3
  10.4 0.0 copy-start.5
  10.4 1.6 fusion.9
  12.0 42.4 %all-gather.14.cloned.1.call-done = bf16[1,256,4096]{2,1,0:T(8,128)(2,1)} async-done(((bf16[1,16,4096]{2,1,0:T(8,128)(2,1)}), bf16[1,256,4096]{2,1,0:T(8,128)(2,1)}) %all-gather.14.cloned.1.call-update) | async-done | bytes 2097168 | tf_op jit(solution)/shard_map/all_gather | solution.py:57
  54.4 2.2 fusion.4
  56.6 0.0 copy-done.5
  56.6 0.0 copy-done
  56.6 7.1 %fusion.22 = (f32[256]{0:T(256)S(1)}, f32[256,1280]{1,0:T(8,128)S(1)}) fusion(bf16[1,4096,1280]{2,1,0:T(8,128)(2,1)} %param.14, bf16[1,256,4096]{2,1,0:T(8,128)(2,1)S(1)} %copy-done, f32[4096]{0:T(1024)S(1)} %bitcast.78, f32[256]{0:T(256)S(1)} %add_rsqrt_fusion), kind=kOutput, calls=%fused_computation.50 | convolution fusion | flops 2688876288 | bytes 13912064 | tf_op jit(solution)/shard_map/dot_general | solution.py:59
  63.7 0.3 fusion.14
  64.0 19.1 %all-gather.8 = f32[16,1,256]{2,1,0:T(1,128)S(1)} all-gather(f32[1,1,256]{2,1,0:T(1,128)S(1)} %bitcast.76), channel_id=6, replica_groups=mesh['branch'=2,'tok'=16] {'tok'}, dimensions={0}, use_global_device_ids=true | all-gather | bytes 17408 | tf_op jit(solution)/shard_map/all_gather | solution.py:13
  83.1 17.4 %all-gather.7 = f32[16,1,256]{2,1,0:T(1,128)S(1)} all-gather(f32[1,1,256]{2,1,0:T(1,128)S(1)} %bitcast.71), channel_id=5, replica_groups=mesh['branch'=2,'tok'=16] {'tok'}, dimensions={0}, use_global_device_ids=true | all-gather | bytes 17408 | tf_op jit(solution)/shard_map/all_gather | solution.py:13
  100.6 0.8 while.35
  101.4 1.4 divide_multiply_fusion
  102.8 0.0 all-reduce.2.cloned.1.call-update
  102.9 0.0 copy-start.4
  102.9 0.0 reduce-scatter.2.cloned.1.call-start
  102.9 81.2 %all-gather.12.cloned.1.call-done = bf16[4096,1280]{1,0:T(8,128)(2,1)} async-done(((bf16[2048,1280]{1,0:T(8,128)(2,1)}), bf16[4096,1280]{1,0:T(8,128)(2,1)}) %all-gather.12.cloned.1.call-update) | async-done | bytes 10485776 | tf_op jit(solution)/shard_map/all_gather | solution.py:67
  184.1 6.0 %fusion.23 = (f32[128]{0:T(128)S(1)}, f32[128,1280]{1,0:T(8,128)S(1)}) fusion(bf16[128,4096]{0,1:T(8,128)(2,1)} %fusion.9, bf16[4096,1280]{1,0:T(8,128)(2,1)} %all-gather.12.cloned.1.call-done), kind=kOutput, calls=%fused_computation.51 | convolution fusion | flops 1342340992 | bytes 12190208 | tf_op jit(solution)/shard_map/dot_general | solution.py:65
  190.1 0.3 fusion.15
  190.4 21.3 %all-gather.6 = f32[16,1,128]{2,1,0:T(1,128)S(1)} all-gather(f32[1,1,128]{2,1,0:T(1,128)S(1)} %bitcast.77), channel_id=3, replica_groups=mesh['branch'=2,'tok'=16] {'tok'}, dimensions={0}, use_global_device_ids=true | all-gather | bytes 8704 | tf_op jit(solution)/shard_map/all_gather | solution.py:13
  211.7 17.4 %all-gather.5 = f32[16,1,128]{2,1,0:T(1,128)S(1)} all-gather(f32[1,1,128]{2,1,0:T(1,128)S(1)} %bitcast.74), channel_id=2, replica_groups=mesh['branch'=2,'tok'=16] {'tok'}, dimensions={0}, use_global_device_ids=true | all-gather | bytes 8704 | tf_op jit(solution)/shard_map/all_gather | solution.py:13
  229.1 0.7 while.34
  229.8 3.1 all-reduce.2.cloned.1.call-done
  232.9 1.4 multiply_convert_fusion
  234.3 8.7 %fusion.25 = f32[128,4096]{1,0:T(8,128)} fusion(bf16[128,1280]{1,0:T(8,128)(2,1)S(1)} %multiply_convert_fusion, bf16[4096,1280]{1,0:T(8,128)(2,1)} %all-gather.12.cloned.1.call-done), kind=kOutput, calls=%fused_computation.53 | convolution fusion | flops 1342177280 | bytes 12910592 | tf_op jit(solution)/shard_map/dot_general | solution.py:78
  243.0 0.0 reduce-scatter.2.cloned.1.call-update
  243.0 3.6 %all-to-all-start = ((bf16[128,2,2048]{0,2,1:T(8,128)(2,1)}), bf16[128,2,2048]{0,2,1:T(8,128)(2,1)S(1)}, u32[]{:S(2)}, u32[]{:S(2)}) async-start(bf16[128,2,2048]{0,2,1:T(8,128)(2,1)} %bitcast.4), calls=%async_computation | async-start | bytes 2097152 | tf_op jit(solution)/shard_map/all_to_all | solution.py:97
  246.6 0.1 dynamic_slice.50
  246.7 13.6 %all-to-all-done = bf16[128,2,2048]{0,2,1:T(8,128)(2,1)S(1)} async-done(((bf16[128,2,2048]{0,2,1:T(8,128)(2,1)}), bf16[128,2,2048]{0,2,1:T(8,128)(2,1)S(1)}, u32[]{:S(2)}, u32[]{:S(2)}) %all-to-all-start) | async-done | bytes 1048608 | tf_op jit(solution)/shard_map/all_to_all | solution.py:97
  260.3 0.5 copy.14
  260.9 9.1 %all_gather.44 = bf16[256,1280]{1,0:T(8,128)(2,1)S(1)} all-gather(bf16[128,1280]{1,0:T(8,128)(2,1)S(1)} %multiply_convert_fusion), channel_id=1, replica_groups=mesh['branch'=2,'tok'=16] {'branch'}, dimensions={0}, use_global_device_ids=true | all-gather | bytes 983040 | tf_op jit(solution)/shard_map/all_gather | solution.py:98
  269.9 5.7 %fusion.24 = f32[2048,1280]{1,0:T(8,128)} fusion(bf16[256,2048]{1,0:T(8,128)(2,1)S(1)} %bitcast.63, bf16[256,1280]{1,0:T(8,128)(2,1)S(1)} %all_gather.44), kind=kOutput, calls=%fused_computation.52 | convolution fusion | flops 1342177280 | bytes 12189696 | tf_op jit(solution)/shard_map/dot_general | solution.py:99
  275.6 29.3 %reduce-scatter.2.cloned.1.call-done = f32[128,256]{1,0:T(8,128)} async-done(((f32[128,4096]{1,0:T(8,128)}), f32[128,256]{1,0:T(8,128)}) %reduce-scatter.2.cloned.1.call-update) | async-done | bytes 131088 | tf_op jit(solution)/shard_map/reduce_scatter | solution.py:84
  305.0 1.0 fusion.21
  306.0 29.5 %psum.22 = f32[128]{0:T(128)S(1)} all-reduce(f32[128]{0:T(128)S(1)} %get-tuple-element.274), channel_id=1, replica_groups=mesh['branch'=2,'tok'=16] {'tok'}, use_global_device_ids=true, to_apply=%region_13.0 | all-reduce | flops 128 | bytes 1024 | tf_op jit(solution)/shard_map/psum | solution.py:92
  335.5 5.5 %psum.23 = f32[256]{0:T(256)} all-reduce(f32[256]{0:T(256)S(1)} %get-tuple-element.273), channel_id=1, replica_groups=mesh['branch'=2,'tok'=16] {'branch'}, use_global_device_ids=true, to_apply=%region_15.0 | all-reduce | flops 256 | bytes 2048 | tf_op jit(solution)/shard_map/psum | solution.py:91
  341.0 1.7 fusion.18
  (60 shorter events, 0.9 us)
Async XLA Ops:
  7.2 47.2 %all-gather.14.cloned.1.call-start = ((), (), s32[]{:S(2)}) async-start(), calls=%async_computation.5 | async-start | bytes 2228224 | tf_op jit(solution)/shard_map/all_gather | solution.py:57
  7.9 1.2 copy-start.1
  7.9 176.2 %all-gather.12.cloned.1.call-start = ((), (), s32[]{:S(2)}) async-start(), calls=%async_computation.2 | async-start | bytes 15728640 | tf_op jit(solution)/shard_map/all_gather | solution.py:67
  8.7 1.7 copy-start.3
  8.7 1.7 copy-start.2
  8.7 224.2 %all-reduce.2.cloned.1.call-start = ((), (), s32[]{:S(2)}) async-start(), calls=%async_computation.3 | async-start | bytes 2621440 | tf_op jit(solution)/shard_map/psum | solution.py:62
  10.4 46.2 %copy-start.5 = (f32[1,4096]{1,0:T(1,128)S(1)}, f32[1,4096]{1,0:T(1,128)}, u32[]{:S(2)}) copy-start(f32[1,4096]{1,0:T(1,128)} %param.13) | copy-start | bytes 49156
  54.3 2.3 copy-start
  102.9 130.0 %copy-start.4 = (s32[128]{0:T(128)S(1)}, s32[128]{0:T(128)}, u32[]{:S(2)}) copy-start(s32[128]{0:T(128)} %param.19) | copy-start | bytes 1540
  102.9 202.1 %reduce-scatter.2.cloned.1.call-start = ((), (), s32[]{:S(2)}) async-start(), calls=%async_computation.4 | async-start | bytes 2228224 | tf_op jit(solution)/shard_map/reduce_scatter | solution.py:84
  243.0 17.3 %all-to-all-start = ((bf16[128,2,2048]{0,2,1:T(8,128)(2,1)}), bf16[128,2,2048]{0,2,1:T(8,128)(2,1)S(1)}, u32[]{:S(2)}, u32[]{:S(2)}) async-start(bf16[128,2,2048]{0,2,1:T(8,128)(2,1)} %bitcast.4), calls=%async_computation | async-start | bytes 2097152 | tf_op jit(solution)/shard_map/all_to_all | solution.py:97
Sparse Core Ops, SparseCore 0:
  10.1 44.1 all-gather.13
  55.9 128.1 all-gather.11
  187.0 45.8 all-reduce.1
  243.2 61.7 reduce-scatter.1
where the time goes:
time: 350 us; the launch traced here: 349 us
  waiting for transfers between devices  171 us (49%)
  blocking collectives  119 us (34%)
  matrix products  27.5 us (8%)
  between operations  13.9 us (4%)
  other arithmetic  11.2 us (3%)
  starting transfers between devices  3.75 us (1%)
    all_gather x1, waiting for transfers between devices, per_device(): lax.all_gather(student_head, 'branch', axis=0, tiled=True)  81.2 us
    all_gather x4, blocking collectives, merged(): everything = jax.tree.map(lambda part: lax.all_gather(part, axis), value)  75.3 us
    all_gather x1, waiting for transfers between devices, per_device(): lax.all_gather(teacher_hidden[0], 'tok', axis=0, tiled=True)  42.4 us
    psum x1, blocking collectives, per_device(): lax.psum(jnp.sum(gain_cols[None, :] * normed_grads * hidden_cols, axis=1)...  29.5 us
    reduce_scatter x1, waiting for transfers between devices, per_device(): lax.psum_scatter(partial_grads, 'tok', scatter_dimension=1, tiled=True)  29.3 us
    all_to_all x1, waiting for transfers between devices, per_device(): lax.all_to_all(student_normed, 'branch', split_axis=1, concat_axis=0, til...  13.6 us
    all_gather x1, blocking collectives, per_device(): all_grads = lax.all_gather(logit_grads, 'branch', axis=0, tiled=True)  9.09 us
    dot_general x1, matrix products, per_device(): lax.dot_general(logit_grads, lax.all_gather(student_head, 'branch', axis=...  8.73 us
  transfers between devices with their start and end apart: 5, of which 5 were waited for; matrix products, arithmetic and copies ran while one was open for 8% of the time, Pallas kernels for 0%

commit v1 on v0

--- a/solution.py
+++ b/solution.py
@@ -1,3 +1,4 @@
+import functools
 import jax
 import jax.numpy as jnp
 from jax import lax
@@ -7,6 +8,15 @@
 eps = 1e-05
 mix_label = 0.25
 loss_scale = 64.0
+
+
+def launch_counts(patch, axis_id, dim_at):
+    ready = jnp.stack([patch for _ in range(jax.lax.axis_size(axis_id))], 0)
+    x_next = jax.lax.all_to_all(ready, axis_name=axis_id, split_axis=0, concat_axis=0)
+    return jnp.concatenate(x_next, dim_at)
+
+
+remake_rows = functools.partial(launch_counts, axis_id="branch", dim_at=0)
 
 
 def merged(value, axis, combine):
@@ -63,9 +73,7 @@
     mixed = lax.dynamic_slice_in_dim(mixed_all, lax.axis_index("branch") * rows_here, rows_here, 0)
     student_normed, inv_scale = normalize(student_hidden, student_gain)
     student_logits = jnp.dot(
-        student_normed,
-        lax.all_gather(student_head, "branch", axis=0, tiled=True),
-        preferred_element_type=jnp.float32,
+        student_normed, remake_rows(student_head), preferred_element_type=jnp.float32
     )
     student_probs = probabilities(student_logits)
     offset = lax.axis_index("tok") * head_cols

time: 350 us -> 477 us (1.36)
  waiting for transfers between devices: 171 us -> 281 us
  other arithmetic: 11.2 us -> 21.1 us
  starting transfers between devices: 3.75 us -> 11.5 us
    all_to_all x0 -> x1, waiting for transfers between devices: none -> 192 us  [launch_counts(): jax.lax.all_to_all(ready, axis_name=axis_id, split_axis=0, concat_axis=0)]
    all_gather x1, waiting for transfers between devices: 81.2 us -> 0.02 us  [per_device(): lax.all_gather(student_head, 'branch', axis=0, tiled=True)]
    another operation x0 -> x1, other arithmetic: none -> 9.22 us  [launch_counts(): ready = jnp.stack([patch for _ in range(jax.lax.axis_size(axis_id))], 0)]
    all_to_all x0 -> x1, starting transfers between devices: none -> 7.73 us  [launch_counts(): jax.lax.all_to_all(ready, axis_name=axis_id, split_axis=0, concat_axis=0)]
  transfers between devices with their start and end apart: 5 -> 6, of which waited for: 5 -> 4; matrix products, arithmetic and copies ran while one was open for 8% -> 6% of each run, Pallas kernels for 0% -> 0%
where the time goes in v1:
time: 477 us
  waiting for transfers between devices  281 us (59%)
  blocking collectives  119 us (25%)
  matrix products  27.4 us (6%)
  other arithmetic  21.1 us (4%)
  between operations  13.9 us (3%)
  starting transfers between devices  11.5 us (2%)
    all_to_all x1, waiting for transfers between devices, launch_counts(): jax.lax.all_to_all(ready, axis_name=axis_id, split_axis=0, concat_axis=0)  192 us
    all_gather x4, blocking collectives, merged(): everything = jax.tree.map(lambda part: lax.all_gather(part, axis), value)  74.5 us
    all_gather x1, waiting for transfers between devices, per_device(): lax.all_gather(teacher_hidden[0], 'tok', axis=0, tiled=True)  45.7 us
    psum x1, blocking collectives, per_device(): lax.psum(jnp.sum(gain_cols[None, :] * normed_grads * hidden_cols, axis=1)...  29.5 us
    reduce_scatter x1, waiting for transfers between devices, per_device(): lax.psum_scatter(partial_grads, 'tok', scatter_dimension=1, tiled=True)  27.6 us
    all_to_all x1, waiting for transfers between devices, per_device(): lax.all_to_all(student_normed, 'branch', split_axis=1, concat_axis=0, til...  14.3 us
    all_gather x1, blocking collectives, per_device(): all_grads = lax.all_gather(logit_grads, 'branch', axis=0, tiled=True)  9.76 us
  transfers between devices with their start and end apart: 6, of which 4 were waited for; matrix products, arithmetic and copies ran while one was open for 6% of the time, Pallas kernels for 0%

profile of v1, /device:TPU:0, one launch (start us, length us, event | category | flops | bytes accessed | tf_op | source)
XLA Modules:
  0.0 476.7 jit_solution(6709986545892632611)
XLA Ops:
  7.2 0.0 all-gather.14.cloned.1.call-start
  7.2 0.7 all-gather.14.cloned.1.call-update
  7.9 0.0 all-reduce.2.cloned.1.call-start
  8.0 0.7 convert_multiply_fusion.7
  8.6 45.7 %all-gather.14.cloned.1.call-done = bf16[1,256,4096]{2,1,0:T(8,128)(2,1)} async-done(((bf16[1,16,4096]{2,1,0:T(8,128)(2,1)}), bf16[1,256,4096]{2,1,0:T(8,128)(2,1)}) %all-gather.14.cloned.1.call-update) | async-done | bytes 2097168 | tf_op jit(solution)/shard_map/all_gather | solution.py:67
  54.4 2.2 fusion.4
  56.6 0.0 copy-done
  56.6 7.0 %fusion.22 = (f32[256]{0:T(256)S(1)}, f32[256,1280]{1,0:T(8,128)S(1)}) fusion(bf16[1,4096,1280]{2,1,0:T(8,128)(2,1)} %param.14, bf16[1,256,4096]{2,1,0:T(8,128)(2,1)S(1)} %copy-done, f32[4096]{0:T(1024)S(1)} %bitcast.81, f32[256]{0:T(256)S(1)} %add_rsqrt_fusion), kind=kOutput, calls=%fused_computation.51 | convolution fusion | flops 2688876288 | bytes 13912064 | tf_op jit(solution)/shard_map/dot_general | solution.py:69
  63.6 0.3 fusion.14
  64.0 19.2 %all-gather.8 = f32[16,1,256]{2,1,0:T(1,128)S(1)} all-gather(f32[1,1,256]{2,1,0:T(1,128)S(1)} %bitcast.79), channel_id=6, replica_groups=mesh['branch'=2,'tok'=16] {'tok'}, dimensions={0}, use_global_device_ids=true | all-gather | bytes 17408 | tf_op jit(solution)/shard_map/all_gather | solution.py:23
  83.1 17.4 %all-gather.7 = f32[16,1,256]{2,1,0:T(1,128)S(1)} all-gather(f32[1,1,256]{2,1,0:T(1,128)S(1)} %bitcast.74), channel_id=5, replica_groups=mesh['branch'=2,'tok'=16] {'tok'}, dimensions={0}, use_global_device_ids=true | all-gather | bytes 17408 | tf_op jit(solution)/shard_map/all_gather | solution.py:23
  100.6 0.8 while.35
  101.5 1.5 divide_multiply_fusion
  102.9 0.0 all-reduce.2.cloned.1.call-update
  102.9 9.2 %pad_maximum_fusion = bf16[2,2048,1280]{2,1,0:T(8,128)(2,1)} fusion(bf16[1,2048,1280]{2,1,0:T(8,128)(2,1)} %bitcast.65), kind=kLoop, calls=%fused_computation.9 | loop fusion | flops 5242880 | bytes 15728640 | tf_op jit(solution)/shard_map/stack | solution.py:14
  112.2 7.7 %all-to-all-start.1 = ((bf16[2,2048,1280]{2,1,0:T(8,128)(2,1)}), bf16[2,2048,1280]{2,1,0:T(8,128)(2,1)}, u32[]{:S(2)}, u32[]{:S(2)}) async-start(bf16[2,2048,1280]{2,1,0:T(8,128)(2,1)} %pad_maximum_fusion), calls=%async_computation.1 | async-start | bytes 20971520 | tf_op jit(solution)/shard_map/all_to_all | solution.py:15
  119.9 0.0 copy-start.1
  119.9 0.0 all-gather.12.cloned.1.call-start
  120.0 0.7 all-gather.12.cloned.1.call-update
  120.7 0.0 copy-start.2
  120.7 0.0 reduce-scatter.2.cloned.1.call-start
  120.7 0.4 copy-done.1
  121.2 0.7 copy.13
  121.8 0.6 fusion.7
  122.4 1.5 fusion.9
  123.9 192.1 %all-to-all-done.1 = bf16[2,2048,1280]{2,1,0:T(8,128)(2,1)} async-done(((bf16[2,2048,1280]{2,1,0:T(8,128)(2,1)}), bf16[2,2048,1280]{2,1,0:T(8,128)(2,1)}, u32[]{:S(2)}, u32[]{:S(2)}) %all-to-all-start.1) | async-done | bytes 10485792 | tf_op jit(solution)/shard_map/all_to_all | solution.py:15
  316.0 6.0 %fusion.23 = (f32[128]{0:T(128)S(1)}, f32[128,1280]{1,0:T(8,128)S(1)}) fusion(bf16[128,4096]{0,1:T(8,128)(2,1)} %fusion.9, bf16[4096,1280]{1,0:T(8,128)(2,1)} %bitcast.8), kind=kOutput, calls=%fused_computation.52 | convolution fusion | flops 1342340992 | bytes 12190208 | tf_op jit(solution)/shard_map/dot_general | solution.py:75
  322.0 0.3 fusion.15
  322.3 20.4 %all-gather.6 = f32[16,1,128]{2,1,0:T(1,128)S(1)} all-gather(f32[1,1,128]{2,1,0:T(1,128)S(1)} %bitcast.80), channel_id=3, replica_groups=mesh['branch'=2,'tok'=16] {'tok'}, dimensions={0}, use_global_device_ids=true | all-gather | bytes 8704 | tf_op jit(solution)/shard_map/all_gather | solution.py:23
  342.7 17.4 %all-gather.5 = f32[16,1,128]{2,1,0:T(1,128)S(1)} all-gather(f32[1,1,128]{2,1,0:T(1,128)S(1)} %bitcast.77), channel_id=2, replica_groups=mesh['branch'=2,'tok'=16] {'tok'}, dimensions={0}, use_global_device_ids=true | all-gather | bytes 8704 | tf_op jit(solution)/shard_map/all_gather | solution.py:23
  360.1 0.7 while.34
  360.8 0.0 all-reduce.2.cloned.1.call-done
  360.8 0.0 copy-done.3
  360.8 1.4 multiply_convert_fusion
  362.2 0.0 all-gather.12.cloned.1.call-done
  362.3 8.7 %fusion.25 = f32[128,4096]{1,0:T(8,128)} fusion(bf16[128,1280]{1,0:T(8,128)(2,1)S(1)} %multiply_convert_fusion, bf16[4096,1280]{1,0:T(8,128)(2,1)} %all-gather.12.cloned.1.call-done), kind=kOutput, calls=%fused_computation.54 | convolution fusion | flops 1342177280 | bytes 12910592 | tf_op jit(solution)/shard_map/dot_general | solution.py:86
  371.0 0.0 reduce-scatter.2.cloned.1.call-update
  371.0 3.6 all-to-all-start
  374.6 0.1 dynamic_slice.50
  374.7 14.3 %all-to-all-done = bf16[128,2,2048]{0,2,1:T(8,128)(2,1)S(1)} async-done(((bf16[128,2,2048]{0,2,1:T(8,128)(2,1)}), bf16[128,2,2048]{0,2,1:T(8,128)(2,1)S(1)}, u32[]{:S(2)}, u32[]{:S(2)}) %all-to-all-start) | async-done | bytes 1048608 | tf_op jit(solution)/shard_map/all_to_all | solution.py:105
  389.0 0.5 copy.14
  389.5 9.8 %all_gather.42 = bf16[256,1280]{1,0:T(8,128)(2,1)S(1)} all-gather(bf16[128,1280]{1,0:T(8,128)(2,1)S(1)} %multiply_convert_fusion), channel_id=1, replica_groups=mesh['branch'=2,'tok'=16] {'branch'}, dimensions={0}, use_global_device_ids=true | all-gather | bytes 983040 | tf_op jit(solution)/shard_map/all_gather | solution.py:106
  399.3 5.7 %fusion.24 = f32[2048,1280]{1,0:T(8,128)} fusion(bf16[256,2048]{1,0:T(8,128)(2,1)S(1)} %bitcast.66, bf16[256,1280]{1,0:T(8,128)(2,1)S(1)} %all_gather.42), kind=kOutput, calls=%fused_computation.53 | convolution fusion | flops 1342177280 | bytes 12189696 | tf_op jit(solution)/shard_map/dot_general | solution.py:107
  404.9 27.6 %reduce-scatter.2.cloned.1.call-done = f32[128,256]{1,0:T(8,128)} async-done(((f32[128,4096]{1,0:T(8,128)}), f32[128,256]{1,0:T(8,128)}) %reduce-scatter.2.cloned.1.call-update) | async-done | bytes 131088 | tf_op jit(solution)/shard_map/reduce_scatter | solution.py:92
  432.5 1.0 fusion.21
  433.6 29.5 %psum.22 = f32[128]{0:T(128)S(1)} all-reduce(f32[128]{0:T(128)S(1)} %get-tuple-element.274), channel_id=1, replica_groups=mesh['branch'=2,'tok'=16] {'tok'}, use_global_device_ids=true, to_apply=%region_13.0 | all-reduce | flops 128 | bytes 1024 | tf_op jit(solution)/shard_map/psum | solution.py:100
  463.1 5.5 %psum.23 = f32[256]{0:T(256)} all-reduce(f32[256]{0:T(256)S(1)} %get-tuple-element.273), channel_id=1, replica_groups=mesh['branch'=2,'tok'=16] {'branch'}, use_global_device_ids=true, to_apply=%region_15.0 | all-reduce | flops 256 | bytes 2048 | tf_op jit(solution)/shard_map/psum | solution.py:99
  468.5 1.7 fusion.18
  (61 shorter events, 0.9 us)
Async XLA Ops:
  7.2 49.4 %copy-start.4 = (f32[1,4096]{1,0:T(1,128)S(1)}, f32[1,4096]{1,0:T(1,128)}, u32[]{:S(2)}) copy-start(f32[1,4096]{1,0:T(1,128)} %param.13) | copy-start | bytes 49156
  7.2 47.2 %all-gather.14.cloned.1.call-start = ((), (), s32[]{:S(2)}) async-start(), calls=%async_computation.6 | async-start | bytes 2228224 | tf_op jit(solution)/shard_map/all_gather | solution.py:67
  7.9 352.9 %all-reduce.2.cloned.1.call-start = ((), (), s32[]{:S(2)}) async-start(), calls=%async_computation.3 | async-start | bytes 2621440 | tf_op jit(solution)/shard_map/psum | solution.py:72
  54.4 2.3 copy-start
  112.2 203.9 %all-to-all-start.1 = ((bf16[2,2048,1280]{2,1,0:T(8,128)(2,1)}), bf16[2,2048,1280]{2,1,0:T(8,128)(2,1)}, u32[]{:S(2)}, u32[]{:S(2)}) async-start(bf16[2,2048,1280]{2,1,0:T(8,128)(2,1)} %pad_maximum_fusion), calls=%async_computation.1 | async-start | bytes 20971520 | tf_op jit(solution)/shard_map/all_to_all | solution.py:15
  119.9 1.2 copy-start.1
  119.9 242.3 %all-gather.12.cloned.1.call-start = ((), (), s32[]{:S(2)}) async-start(), calls=%async_computation.4 | async-start | bytes 15728640 | tf_op jit(solution)/shard_map/all_gather | solution.py:88
  120.7 1.7 copy-start.2
  120.7 311.9 %reduce-scatter.2.cloned.1.call-start = ((), (), s32[]{:S(2)}) async-start(), calls=%async_computation.5 | async-start | bytes 2228224 | tf_op jit(solution)/shard_map/reduce_scatter | solution.py:92
  316.0 44.8 %copy-start.3 = (s32[128]{0:T(128)S(1)}, s32[128]{0:T(128)}, u32[]{:S(2)}) copy-start(s32[128]{0:T(128)} %param.19) | copy-start | bytes 1540
  371.0 18.0 %all-to-all-start = ((bf16[128,2,2048]{0,2,1:T(8,128)(2,1)}), bf16[128,2,2048]{0,2,1:T(8,128)(2,1)S(1)}, u32[]{:S(2)}, u32[]{:S(2)}) async-start(bf16[128,2,2048]{0,2,1:T(8,128)(2,1)} %bitcast.4), calls=%async_computation | async-start | bytes 2097152 | tf_op jit(solution)/shard_map/all_to_all | solution.py:105
Sparse Core Ops, SparseCore 0:
  10.1 44.1 all-gather.13
  103.1 61.9 all-reduce.1
  166.6 195.3 all-gather.11
  371.1 61.3 reduce-scatter.1
